TPU v7x, 256 devices: a whole 4x4x8 slice. The times are simulated.
256 devices in a mesh: lat: 4 (over y_lo, core), lon: 16 (over y_hi, z), ch: 4 (over x).
Axes of the slice: x: 4, y: 4 (y_hi: 2, y_lo: 2; y = y_hi * 2 + y_lo), z: 8, core: 2. Of those that a mesh axis runs over, the one named last changes fastest.
Arguments:
- grid_field: bfloat16 [1440, 4, 49152], P('lon', 'ch', 'lat'), may hold values from -6 to 6
- first_weight: bfloat16 [4, 2, 96, 96], P('ch'), may hold values from -0.4375 to 0.4375
- first_bias: float32 [4, 2, 96], P('ch'), may hold values from -3 to 3
- second_weight: bfloat16 [4, 2, 96, 96], P('ch'), may hold values from -0.4375 to 0.4375
- second_bias: float32 [4, 2, 96], P('ch'), may hold values from -3 to 3
Outputs:
- mixed: bfloat16 [1440, 4, 49152], P('lon', 'ch', 'lat')
All inputs are finite; a program needn't handle non-finite values.
Results may differ from a plain program's by a relative error of at most 0.0073.
Values may be sent and summed in bfloat16 or wider, within the bound.
No kernel may reach another device: no remote copies, remote signals or barrier semaphores. Data moves between devices by JAX's collectives and lax.ppermute only.
A program may use at most 128 MiB of HBM per device.

v0:
```python
import math
import jax
import jax.numpy as jnp
from jax import lax
from jax.sharding import PartitionSpec as P

shrink_level = 0.01


def phase_tables(length):
    indices = jnp.arange(length, dtype=jnp.int32)
    product = indices[:, None] * indices[None, :] % length
    angles = product.astype(jnp.float32) * (2.0 * math.pi / length)
    return (jnp.cos(angles), jnp.sin(angles))


def lon_tables(length):
    cosine_tab, sine_tab = phase_tables(length)
    kept_modes = length // 2
    factor = 1.0 / math.sqrt(length)
    forward = jnp.concatenate([cosine_tab[:kept_modes], -sine_tab[:kept_modes]], axis=0) * factor
    weights = jnp.where(jnp.arange(kept_modes) == 0, 1.0, 2.0).astype(jnp.float32)
    inverse = (
        jnp.concatenate(
            [cosine_tab[:, :kept_modes] * weights, -sine_tab[:, :kept_modes] * weights], axis=1
        )
        * factor
    )
    return (forward.astype(jnp.bfloat16), inverse.astype(jnp.bfloat16))


def lat_tables(length):
    cosine_tab, sine_tab = phase_tables(length)
    factor = 1.0 / math.sqrt(length)
    forward = (
        jnp.stack(
            [jnp.stack([cosine_tab, sine_tab], axis=1), jnp.stack([-sine_tab, cosine_tab], axis=1)],
            axis=0,
        )
        * factor
    )
    inverse = (
        jnp.stack(
            [jnp.stack([cosine_tab, -sine_tab], axis=1), jnp.stack([sine_tab, cosine_tab], axis=1)],
            axis=0,
        )
        * factor
    )
    return (forward.astype(jnp.bfloat16), inverse.astype(jnp.bfloat16))


def complex_blocks(weight):
    real_part, imag_part = (weight[:, 0], weight[:, 1])
    return jnp.stack(
        [jnp.stack([real_part, imag_part], axis=2), jnp.stack([-imag_part, real_part], axis=2)],
        axis=1,
    )


def block_mixing(mode_data, first_weight, first_bias, second_weight, second_bias):
    shape = mode_data.shape
    blocks_here = first_weight.shape[0]
    block_width = first_weight.shape[2]
    split_data = mode_data.reshape(shape[0], shape[1], shape[2], blocks_here, block_width)
    hidden = jnp.einsum(
        "rkqbc,brcsd->skqbd",
        split_data,
        complex_blocks(first_weight),
        preferred_element_type=jnp.float32,
    )
    hidden = jax.nn.relu(hidden + jnp.moveaxis(first_bias, 1, 0)[:, None, None, :, :]).astype(
        jnp.bfloat16
    )
    output = jnp.einsum(
        "rkqbc,brcsd->skqbd",
        hidden,
        complex_blocks(second_weight),
        preferred_element_type=jnp.float32,
    )
    output = output + jnp.moveaxis(second_bias, 1, 0)[:, None, None, :, :]
    shrunk = jnp.sign(output) * jnp.maximum(jnp.abs(output) - shrink_level, 0.0)
    return shrunk.astype(jnp.bfloat16).reshape(shape)


def lat_apply(data, table):
    columns = lax.all_to_all(data, "lat", split_axis=3, concat_axis=2, tiled=True)
    result = jnp.einsum(
        "sqrh,rkhc->skqc", table, columns, preferred_element_type=jnp.float32
    ).astype(jnp.bfloat16)
    return lax.all_to_all(result, "lat", split_axis=2, concat_axis=3, tiled=True)


def per_device(grid_field, first_weight, first_bias, second_weight, second_bias):
    lon_devices = lax.axis_size("lon")
    lat_devices = lax.axis_size("lat")
    block_width = first_weight.shape[2]
    local_lon, blocks_here, merged = grid_field.shape
    local_lat = merged // block_width
    local_chan = blocks_here * block_width
    lon_size = local_lon * lon_devices
    lat_size = local_lat * lat_devices
    kept_modes = lon_size // 2
    lon_forward, lon_inverse = lon_tables(lon_size)
    lat_forward, lat_inverse = lat_tables(lat_size)
    reordered = grid_field.reshape(local_lon, blocks_here, local_lat, block_width).transpose(
        0, 2, 1, 3
    )
    flattened = reordered.reshape(local_lon, local_lat * local_chan)
    gathered = lax.all_to_all(flattened, "lon", split_axis=1, concat_axis=0, tiled=True)
    spectra = jnp.dot(lon_forward, gathered, preferred_element_type=jnp.float32).astype(
        jnp.bfloat16
    )
    spectra = spectra.reshape(2, kept_modes, gathered.shape[1])
    spectra = lax.all_to_all(spectra, "lon", split_axis=1, concat_axis=2, tiled=True)
    spectra = spectra.reshape(2, spectra.shape[1], local_lat, local_chan)
    mode_data = lat_apply(spectra, lat_forward)
    shrunk = block_mixing(mode_data, first_weight, first_bias, second_weight, second_bias)
    returned = lat_apply(shrunk, lat_inverse)
    returned = returned.reshape(2, returned.shape[1], local_lat * local_chan)
    returned = lax.all_to_all(returned, "lon", split_axis=2, concat_axis=1, tiled=True)
    columns = returned.reshape(2 * kept_modes, returned.shape[2])
    grid_out = jnp.dot(lon_inverse, columns, preferred_element_type=jnp.float32) + gathered.astype(
        jnp.float32
    )
    grid_out = lax.all_to_all(
        grid_out.astype(jnp.bfloat16), "lon", split_axis=0, concat_axis=1, tiled=True
    )
    grid_out = grid_out.reshape(local_lon, local_lat, blocks_here, block_width).transpose(
        0, 2, 1, 3
    )
    return grid_out.reshape(grid_field.shape)


def solution(mesh):
    in_specs = (
        P("lon", "ch", "lat"),
        P("ch", None, None, None),
        P("ch", None, None),
        P("ch", None, None, None),
        P("ch", None, None),
    )
    out_specs = P("lon", "ch", "lat")
    return jax.shard_map(
        per_device, mesh=mesh, in_specs=in_specs, out_specs=out_specs, check_vma=False
    )
```

profile of v0, /device:TPU:38, one launch (start us, length us, event | category | flops | bytes accessed | tf_op | source)
XLA Modules:
  0.0 631.3 jit_solution(6902518026747214721)
XLA Ops:
  4.5 11.2 %all-to-all-start = ((bf16[90,16,768]{2,0,1:T(8,128)(2,1)}), bf16[90,16,768]{2,0,1:T(8,128)(2,1)S(1)}, u32[]{:S(2)}, u32[]{:S(2)}) async-start(bf16[90,16,768]{2,0,1:T(8,128)(2,1)} %copy.81), calls=%async_computation | async-start | bytes 4718592 | tf_op jit(solution)/shard_map/all_to_all | solution.py:109
  15.7 36.9 %fusion.6 = (f32[1440,1440]{1,0:T(8,128)S(1)}, f32[1440,1440]{1,0:T(8,128)S(1)}) fusion(), kind=kLoop, calls=%fused_computation.10 | loop fusion | flops 18662400 | bytes 16588800 | tf_op jit(solution)/shard_map/sin | solution.py:14
  62.4 8.7 %all-to-all-done = bf16[90,16,768]{2,0,1:T(8,128)(2,1)S(1)} async-done(((bf16[90,16,768]{2,0,1:T(8,128)(2,1)}), bf16[90,16,768]{2,0,1:T(8,128)(2,1)S(1)}, u32[]{:S(2)}, u32[]{:S(2)}) %all-to-all-start) | async-done | bytes 2211872 | tf_op jit(solution)/shard_map/all_to_all | solution.py:109
  73.2 7.8 %fusion.20 = bf16[1440,768]{1,0:T(8,128)(2,1)S(1)} fusion(bf16[1440,768]{1,0:T(8,128)(2,1)} %all_to_all.99, f32[720,1440]{1,0:T(8,128)} %slice_negate_fusion, f32[720,1440]{1,0:T(8,128)} %slice.34), kind=kOutput, calls=%fused_computation.33 | convolution fusion | flops 3192376320 | bytes 12718080 | tf_op jit(solution)/shard_map/dot_general | solution.py:110
  82.8 61.5 %all_to_all.131 = bf16[2,720,768]{2,0,1:T(2,128)(2,1)S(1)} all-to-all(bf16[2,720,768]{2,0,1:T(2,128)(2,1)S(1)} %copy.82), channel_id=1, replica_groups=mesh['lat'=4,'lon'=16,'ch'=4] {'lon'}, dimensions={1} | all-to-all | bytes 4423680 | tf_op jit(solution)/shard_map/all_to_all | solution.py:114
  171.1 14.9 %all-to-all-done.2 = bf16[2,45,128,96]{2,0,1,3:T(2,128)(2,1)S(1)} async-done(((bf16[2,45,128,96]{2,0,1,3:T(2,128)(2,1)}), bf16[2,45,128,96]{2,0,1,3:T(2,128)(2,1)S(1)}, u32[]{:S(2)}, u32[]{:S(2)}) %all-to-all-start.2) | async-done | bytes 2211872 | tf_op jit(solution)/shard_map/all_to_all | solution.py:86
  195.5 8.2 %copy.87 = bf16[2,45,512,24]{1,3,0,2:T(8,128)(2,1)} copy(bf16[2,45,512,24]{2,3,0,1:T(8,128)(2,1)S(1)} %fusion.26) | data formatting | bytes 4423680 | tf_op jit(solution)/shard_map/convert_element_type | solution.py:89
  203.7 13.5 %reshape.178 = bf16[4,2,138240]{2,1,0:T(2,128)(2,1)} reshape(bf16[512,2,24,45]{3,2,1,0:T(8,128)(2,1)} %bitcast.156) | data formatting | bytes 4423680
  221.8 26.3 %all-to-all-done.3 = bf16[4,2,138240]{2,1,0:T(2,128)(2,1)S(1)} async-done(((bf16[4,2,138240]{2,1,0:T(2,128)(2,1)}), bf16[4,2,138240]{2,1,0:T(2,128)(2,1)S(1)}, u32[]{:S(2)}, u32[]{:S(2)}) %all-to-all-start.3) | async-done | bytes 2211872 | tf_op jit(solution)/shard_map/all_to_all | solution.py:90
  248.1 19.2 %reshape.179 = bf16[512,2,24,45]{3,2,1,0:T(8,128)(2,1)} reshape(bf16[4,2,138240]{2,1,0:T(2,128)(2,1)S(1)} %all-to-all-done.3) | data formatting | bytes 4423680
  267.3 7.8 %copy.88 = bf16[2,45,4,128,24]{3,4,2,0,1:T(8,128)(2,1)S(1)} copy(bf16[2,45,4,128,24]{1,4,0,3,2:T(8,128)(2,1)} %bitcast.157) | data formatting | bytes 4423680 | tf_op jit(solution)/shard_map/all_to_all | solution.py:90
  279.9 29.8 %all_to_all.132 = bf16[2,45,128,96]{2,0,1,3:T(2,128)(2,1)S(1)} all-to-all(bf16[2,45,128,96]{2,0,1,3:T(2,128)(2,1)S(1)} %copy.90), channel_id=1, replica_groups=mesh['lat'=4,'lon'=16,'ch'=4] {'lat'}, dimensions={3} | all-to-all | bytes 4423680 | tf_op jit(solution)/shard_map/all_to_all | solution.py:86
  318.6 8.2 %copy.92 = bf16[2,45,512,24]{1,3,0,2:T(8,128)(2,1)} copy(bf16[2,45,512,24]{2,3,0,1:T(8,128)(2,1)S(1)} %fusion.28) | data formatting | bytes 4423680 | tf_op jit(solution)/shard_map/convert_element_type | solution.py:89
  326.8 12.6 %reshape.180 = bf16[4,2,138240]{2,1,0:T(2,128)(2,1)S(1)} reshape(bf16[512,2,24,45]{3,2,1,0:T(8,128)(2,1)} %bitcast.158) | data formatting | bytes 4423680
  339.5 30.3 %all_to_all.133 = bf16[4,2,138240]{2,1,0:T(2,128)(2,1)} all-to-all(bf16[4,2,138240]{2,1,0:T(2,128)(2,1)S(1)} %reshape.180), channel_id=1, replica_groups=mesh['lat'=4,'lon'=16,'ch'=4] {'lat'}, dimensions={0} | all-to-all | bytes 4423680 | tf_op jit(solution)/shard_map/all_to_all | solution.py:90
  369.8 20.1 %reshape.181 = bf16[512,2,24,45]{3,2,1,0:T(8,128)(2,1)} reshape(bf16[4,2,138240]{2,1,0:T(2,128)(2,1)} %all_to_all.133) | data formatting | bytes 4423680
  393.8 52.8 %copy.122 = bf16[2,45,12288]{1,0,2:T(2,128)(2,1)} copy(bf16[2,45,12288]{1,2,0:T(8,128)(2,1)S(1)} %bitcast.154) | data formatting | bytes 4423680 | tf_op jit(solution)/shard_map/reshape | solution.py:119
  446.5 12.6 %reshape.182 = bf16[16,2,34560]{2,1,0:T(2,128)(2,1)} reshape(bf16[12288,2,45]{2,1,0:T(2,128)(2,1)} %bitcast.155) | data formatting | bytes 4423680
  463.8 7.7 %slice_multiply_fusion = (f32[1440,720]{1,0:T(8,128)}, f32[1440,720]{1,0:T(8,128)}) fusion(f32[1440,1440]{1,0:T(8,128)} %copy-done.1, f32[720]{0:T(1024)S(1)} %fusion.69, f32[1440,1440]{1,0:T(8,128)} %copy-done), kind=kLoop, calls=%fused_computation.18 | loop fusion | flops 3110400 | bytes 16591680 | tf_op jit(solution)/shard_map/mul | solution.py:25
  471.5 45.1 %all-to-all-done.6 = bf16[16,2,34560]{2,1,0:T(2,128)(2,1)S(1)} async-done(((bf16[16,2,34560]{2,1,0:T(2,128)(2,1)}), bf16[16,2,34560]{2,1,0:T(2,128)(2,1)S(1)}, u32[]{:S(2)}, u32[]{:S(2)}) %all-to-all-start.6) | async-done | bytes 2211872 | tf_op jit(solution)/shard_map/all_to_all | solution.py:120
  516.6 18.6 %reshape.183 = bf16[12288,2,45]{2,1,0:T(2,128)(2,1)} reshape(bf16[16,2,34560]{2,1,0:T(2,128)(2,1)S(1)} %all-to-all-done.6) | data formatting | bytes 4423680
  535.2 14.6 %copy.107 = bf16[2,45,16,768]{3,1,2,0:T(8,128)(2,1)S(1)} copy(bf16[2,45,16,768]{1,0,3,2:T(2,128)(2,1)} %bitcast.159) | data formatting | bytes 4423680 | tf_op jit(solution)/shard_map/all_to_all | solution.py:120
  552.0 10.0 %add_convert_fusion = bf16[1440,768]{1,0:T(8,128)(2,1)} fusion(bf16[1440,768]{1,0:T(8,128)(2,1)} %all_to_all.99, bf16[1440,768]{1,0:T(8,128)(2,1)} %reshape.163, f32[1440,720]{1,0:T(8,128)} %get-tuple-element.20, f32[1440,720]{1,0:T(8,128)} %get-tuple-element.19), kind=kOutput, calls=%fused_computation.26 | convolution fusion | flops 3194588160 | bytes 14929920 | tf_op jit(solution)/shard_map/dot_general | solution.py:122
  564.6 62.8 %all_to_all.134 = bf16[16,90,768]{2,1,0:T(8,128)(2,1)S(1)} all-to-all(bf16[16,90,768]{2,1,0:T(8,128)(2,1)S(1)} %all_to_all.120), channel_id=1, replica_groups=mesh['lat'=4,'lon'=16,'ch'=4] {'lon'}, dimensions={0} | all-to-all | bytes 4423680 | tf_op jit(solution)/shard_map/all_to_all | solution.py:125
  (54 shorter events, 89.5 us)
Async XLA Ops:
  4.5 66.6 %all-to-all-start = ((bf16[90,16,768]{2,0,1:T(8,128)(2,1)}), bf16[90,16,768]{2,0,1:T(8,128)(2,1)S(1)}, u32[]{:S(2)}, u32[]{:S(2)}) async-start(bf16[90,16,768]{2,0,1:T(8,128)(2,1)} %copy.81), calls=%async_computation | async-start | bytes 4718592 | tf_op jit(solution)/shard_map/all_to_all | solution.py:109
  52.6 3.4 copy-start.1
  52.6 7.3 %copy-start = (f32[1440,1440]{1,0:T(8,128)}, f32[1440,1440]{1,0:T(8,128)S(1)}, u32[]{:S(2)}) copy-start(f32[1440,1440]{1,0:T(8,128)S(1)} %get-tuple-element.23) | copy-start | bytes 24883204
  155.4 30.6 %all-to-all-start.2 = ((bf16[2,45,128,96]{2,0,1,3:T(2,128)(2,1)}), bf16[2,45,128,96]{2,0,1,3:T(2,128)(2,1)S(1)}, u32[]{:S(2)}, u32[]{:S(2)}) async-start(bf16[2,45,128,96]{2,0,1,3:T(2,128)(2,1)} %copy.84), calls=%async_computation.2 | async-start | bytes 4423680 | tf_op jit(solution)/shard_map/all_to_all | solution.py:86
  217.2 4.0 copy-start.2
  217.2 4.3 copy-start.3
  217.2 30.9 %all-to-all-start.3 = ((bf16[4,2,138240]{2,1,0:T(2,128)(2,1)}), bf16[4,2,138240]{2,1,0:T(2,128)(2,1)S(1)}, u32[]{:S(2)}, u32[]{:S(2)}) async-start(bf16[4,2,138240]{2,1,0:T(2,128)(2,1)} %reshape.178), calls=%async_computation.3 | async-start | bytes 4423680 | tf_op jit(solution)/shard_map/all_to_all | solution.py:90
  267.3 7.8 %copy-start.4 = (f32[1,2,96]{2,1,0:T(2,128)S(1)}, f32[1,2,96]{2,1,0:T(2,128)}, u32[]{:S(2)}) copy-start(f32[1,2,96]{2,1,0:T(2,128)} %param.7) | copy-start | bytes 2308
  275.1 0.8 copy-start.5
  459.1 57.5 %all-to-all-start.6 = ((bf16[16,2,34560]{2,1,0:T(2,128)(2,1)}), bf16[16,2,34560]{2,1,0:T(2,128)(2,1)S(1)}, u32[]{:S(2)}, u32[]{:S(2)}) async-start(bf16[16,2,34560]{2,1,0:T(2,128)(2,1)} %reshape.182), calls=%async_computation.6 | async-start | bytes 4423680 | tf_op jit(solution)/shard_map/all_to_all | solution.py:120
where the time goes:
time: 643 us; the launch traced here: 631 us
  local copies, waits for them, and re-layouts  237 us (37%)
  blocking collectives  184 us (29%)
  waiting for transfers between devices  94.9 us (15%)
  other arithmetic  59.1 us (9%)
  matrix products  31.7 us (5%)
  starting transfers between devices  23.6 us (4%)
    unnamed x23, local copies, waits for them, and re-layouts  104 us
    all_to_all x1, blocking collectives, per_device(): lax.all_to_all(grid_out.astype(jnp.bfloat16), 'lon', split_axis=0, concat...  62.8 us
    all_to_all x1, blocking collectives, per_device(): lax.all_to_all(spectra, 'lon', split_axis=1, concat_axis=2, tiled=True)  61.5 us
    reshape x1, local copies, waits for them, and re-layouts, per_device(): returned = returned.reshape(2, returned.shape[1], local_lat * local_chan)  52.8 us
    all_to_all x1, waiting for transfers between devices, per_device(): lax.all_to_all(returned, 'lon', split_axis=2, concat_axis=1, tiled=True)  45.1 us
    sin x2, other arithmetic, phase_tables(): return (jnp.cos(angles), jnp.sin(angles))  40.9 us
    all_to_all x1, blocking collectives, lat_apply(): lax.all_to_all(result, 'lat', split_axis=2, concat_axis=3, tiled=True)  30.3 us
    all_to_all x1, blocking collectives, lat_apply(): lax.all_to_all(data, 'lat', split_axis=3, concat_axis=2, tiled=True)  29.8 us
  transfers between devices with their start and end apart: 4, of which 4 were waited for; matrix products, arithmetic and copies ran while one was open for 10% of the time, Pallas kernels for 0%

commit v1 on v0

--- a/solution.py
+++ b/solution.py
@@ -117,7 +117,9 @@
     shrunk = block_mixing(mode_data, first_weight, first_bias, second_weight, second_bias)
     returned = lat_apply(shrunk, lat_inverse)
     returned = returned.reshape(2, returned.shape[1], local_lat * local_chan)
-    returned = lax.all_to_all(returned, "lon", split_axis=2, concat_axis=1, tiled=True)
+    shards = jnp.split(returned, lax.axis_size("lon"), axis=2)
+    incoming = lax.all_to_all(jnp.stack(shards), "lon", 0, 0)
+    returned = jnp.concatenate(incoming, axis=1)
     columns = returned.reshape(2 * kept_modes, returned.shape[2])
     grid_out = jnp.dot(lon_inverse, columns, preferred_element_type=jnp.float32) + gathered.astype(
         jnp.float32

time: 643 us -> 570 us (0.89)
  local copies, waits for them, and re-layouts: 237 us -> 164 us
    reshape x2 -> x1, local copies, waits for them, and re-layouts: 55 us -> 1.94 us  [per_device(): returned = jnp.concatenate(incoming, axis=1)]
    unnamed x23 -> x38, local copies, waits for them, and re-layouts: 104 us -> 85.5 us
    all_to_all x1 -> x0, local copies, waits for them, and re-layouts: 14.6 us -> none  [per_device(): lax.all_to_all(returned, 'lon', split_axis=2, concat_axis=1, tiled=True)]
    another operation x0 -> x3, local copies, waits for them, and re-layouts: none -> 12.7 us  [the longest x2 10.4 us: per_device(): incoming = lax.all_to_all(jnp.stack(shards), 'lon', 0, 0)]
  transfers between devices with their start and end apart: 4 -> 4, of which waited for: 4 -> 4; matrix products, arithmetic and copies ran while one was open for 10% -> 11% of each run, Pallas kernels for 0% -> 0%
where the time goes in v1:
time: 570 us; the launch traced here: 558 us
  blocking collectives  184 us (32%)
  local copies, waits for them, and re-layouts  164 us (29%)
  waiting for transfers between devices  95.3 us (17%)
  other arithmetic  58.8 us (10%)
  matrix products  31.7 us (6%)
  starting transfers between devices  23.8 us (4%)
    unnamed x38, local copies, waits for them, and re-layouts  85.5 us
    all_to_all x1, blocking collectives, per_device(): lax.all_to_all(grid_out.astype(jnp.bfloat16), 'lon', split_axis=0, concat...  62.8 us
    all_to_all x1, blocking collectives, per_device(): lax.all_to_all(spectra, 'lon', split_axis=1, concat_axis=2, tiled=True)  61.5 us
    all_to_all x1, waiting for transfers between devices, per_device(): incoming = lax.all_to_all(jnp.stack(shards), 'lon', 0, 0)  45.2 us
    sin x2, other arithmetic, phase_tables(): return (jnp.cos(angles), jnp.sin(angles))  40.7 us
    all_to_all x1, blocking collectives, lat_apply(): lax.all_to_all(result, 'lat', split_axis=2, concat_axis=3, tiled=True)  30.1 us
    all_to_all x1, blocking collectives, lat_apply(): lax.all_to_all(data, 'lat', split_axis=3, concat_axis=2, tiled=True)  29.6 us
    all_to_all x1, waiting for transfers between devices, lat_apply(): lax.all_to_all(result, 'lat', split_axis=2, concat_axis=3, tiled=True)  26.3 us
  transfers between devices with their start and end apart: 4, of which 4 were waited for; matrix products, arithmetic and copies ran while one was open for 11% of the time, Pallas kernels for 0%

profile of v1, /device:TPU:38, one launch (start us, length us, event | category | flops | bytes accessed | tf_op | source)
XLA Modules:
  0.0 558.5 jit_solution(2583909220617753023)
XLA Ops:
  4.5 11.2 %all-to-all-start = ((bf16[90,16,768]{2,0,1:T(8,128)(2,1)}), bf16[90,16,768]{2,0,1:T(8,128)(2,1)S(1)}, u32[]{:S(2)}, u32[]{:S(2)}) async-start(bf16[90,16,768]{2,0,1:T(8,128)(2,1)} %copy.132), calls=%async_computation | async-start | bytes 4718592 | tf_op jit(solution)/shard_map/all_to_all | solution.py:109
  15.7 36.6 %fusion.6 = (f32[1440,1440]{1,0:T(8,128)S(1)}, f32[1440,1440]{1,0:T(8,128)S(1)}) fusion(), kind=kLoop, calls=%fused_computation.10 | loop fusion | flops 18662400 | bytes 16588800 | tf_op jit(solution)/shard_map/sin | solution.py:14
  62.2 9.0 %all-to-all-done = bf16[90,16,768]{2,0,1:T(8,128)(2,1)S(1)} async-done(((bf16[90,16,768]{2,0,1:T(8,128)(2,1)}), bf16[90,16,768]{2,0,1:T(8,128)(2,1)S(1)}, u32[]{:S(2)}, u32[]{:S(2)}) %all-to-all-start) | async-done | bytes 2211872 | tf_op jit(solution)/shard_map/all_to_all | solution.py:109
  73.2 7.8 %fusion.20 = bf16[1440,768]{1,0:T(8,128)(2,1)S(1)} fusion(bf16[1440,768]{1,0:T(8,128)(2,1)} %all_to_all.91, f32[720,1440]{1,0:T(8,128)} %slice_negate_fusion, f32[720,1440]{1,0:T(8,128)} %slice.34), kind=kOutput, calls=%fused_computation.33 | convolution fusion | flops 3192376320 | bytes 12718080 | tf_op jit(solution)/shard_map/dot_general | solution.py:110
  82.8 61.5 %all_to_all.121 = bf16[2,720,768]{2,0,1:T(2,128)(2,1)S(1)} all-to-all(bf16[2,720,768]{2,0,1:T(2,128)(2,1)S(1)} %copy.133), channel_id=1, replica_groups=mesh['lat'=4,'lon'=16,'ch'=4] {'lon'}, dimensions={1} | all-to-all | bytes 4423680 | tf_op jit(solution)/shard_map/all_to_all | solution.py:114
  145.9 5.0 reshape.157
  171.3 14.9 %all-to-all-done.2 = bf16[2,45,128,96]{2,0,1,3:T(2,128)(2,1)S(1)} async-done(((bf16[2,45,128,96]{2,0,1,3:T(2,128)(2,1)}), bf16[2,45,128,96]{2,0,1,3:T(2,128)(2,1)S(1)}, u32[]{:S(2)}, u32[]{:S(2)}) %all-to-all-start.2) | async-done | bytes 2211872 | tf_op jit(solution)/shard_map/all_to_all | solution.py:86
  190.3 5.4 fusion.26
  195.7 8.2 %copy.138 = bf16[2,45,512,24]{1,3,0,2:T(8,128)(2,1)} copy(bf16[2,45,512,24]{2,3,0,1:T(8,128)(2,1)S(1)} %fusion.26) | data formatting | bytes 4423680 | tf_op jit(solution)/shard_map/convert_element_type | solution.py:89
  203.9 13.5 %reshape.177 = bf16[4,2,138240]{2,1,0:T(2,128)(2,1)} reshape(bf16[512,2,24,45]{3,2,1,0:T(8,128)(2,1)} %bitcast.212) | data formatting | bytes 4423680
  222.0 26.3 %all-to-all-done.3 = bf16[4,2,138240]{2,1,0:T(2,128)(2,1)S(1)} async-done(((bf16[4,2,138240]{2,1,0:T(2,128)(2,1)}), bf16[4,2,138240]{2,1,0:T(2,128)(2,1)S(1)}, u32[]{:S(2)}, u32[]{:S(2)}) %all-to-all-start.3) | async-done | bytes 2211872 | tf_op jit(solution)/shard_map/all_to_all | solution.py:90
  248.2 19.3 %reshape.178 = bf16[512,2,24,45]{3,2,1,0:T(8,128)(2,1)} reshape(bf16[4,2,138240]{2,1,0:T(2,128)(2,1)S(1)} %all-to-all-done.3) | data formatting | bytes 4423680
  267.5 7.8 %copy.139 = bf16[2,45,4,128,24]{3,4,2,0,1:T(8,128)(2,1)S(1)} copy(bf16[2,45,4,128,24]{1,4,0,3,2:T(8,128)(2,1)} %bitcast.213) | data formatting | bytes 4423680 | tf_op jit(solution)/shard_map/all_to_all | solution.py:90
  280.1 29.6 %all_to_all.122 = bf16[2,45,128,96]{2,0,1,3:T(2,128)(2,1)S(1)} all-to-all(bf16[2,45,128,96]{2,0,1,3:T(2,128)(2,1)S(1)} %copy.141), channel_id=1, replica_groups=mesh['lat'=4,'lon'=16,'ch'=4] {'lat'}, dimensions={3} | all-to-all | bytes 4423680 | tf_op jit(solution)/shard_map/all_to_all | solution.py:86
  313.2 5.4 fusion.28
  318.6 8.2 %copy.143 = bf16[2,45,512,24]{1,3,0,2:T(8,128)(2,1)} copy(bf16[2,45,512,24]{2,3,0,1:T(8,128)(2,1)S(1)} %fusion.28) | data formatting | bytes 4423680 | tf_op jit(solution)/shard_map/convert_element_type | solution.py:89
  326.8 12.6 %reshape.179 = bf16[4,2,138240]{2,1,0:T(2,128)(2,1)S(1)} reshape(bf16[512,2,24,45]{3,2,1,0:T(8,128)(2,1)} %bitcast.214) | data formatting | bytes 4423680
  339.5 30.1 %all_to_all.123 = bf16[4,2,138240]{2,1,0:T(2,128)(2,1)} all-to-all(bf16[4,2,138240]{2,1,0:T(2,128)(2,1)S(1)} %reshape.179), channel_id=1, replica_groups=mesh['lat'=4,'lon'=16,'ch'=4] {'lat'}, dimensions={0} | all-to-all | bytes 4423680 | tf_op jit(solution)/shard_map/all_to_all | solution.py:90
  369.6 20.1 %reshape.180 = bf16[512,2,24,45]{3,2,1,0:T(8,128)(2,1)} reshape(bf16[4,2,138240]{2,1,0:T(2,128)(2,1)} %all_to_all.123) | data formatting | bytes 4423680
  406.1 9.7 %copy.145 = bf16[16,2,45,768]{3,1,2,0:T(2,128)(2,1)} copy(bf16[16,2,45,768]{2,3,1,0:T(8,128)(2,1)} %fusion.65) | data formatting | bytes 4423680 | tf_op jit(solution)/shard_map/stack | solution.py:121
  420.4 7.7 %slice_multiply_fusion = (f32[1440,720]{1,0:T(8,128)}, f32[1440,720]{1,0:T(8,128)}) fusion(f32[1440,1440]{1,0:T(8,128)} %copy-done.1, f32[720]{0:T(1024)S(1)} %fusion.85, f32[1440,1440]{1,0:T(8,128)} %copy-done), kind=kLoop, calls=%fused_computation.18 | loop fusion | flops 3110400 | bytes 16591680 | tf_op jit(solution)/shard_map/mul | solution.py:25
  428.1 45.2 %all-to-all-done.6 = bf16[16,2,45,768]{3,1,2,0:T(2,128)(2,1)S(1)} async-done(((bf16[16,2,45,768]{3,1,2,0:T(2,128)(2,1)}), bf16[16,2,45,768]{3,1,2,0:T(2,128)(2,1)S(1)}, u32[]{:S(2)}, u32[]{:S(2)}) %all-to-all-start.6) | async-done | bytes 2211872 | tf_op jit(solution)/shard_map/all_to_all | solution.py:121
  478.8 10.0 %add_convert_fusion = bf16[1440,768]{1,0:T(8,128)(2,1)} fusion(bf16[1440,768]{1,0:T(8,128)(2,1)} %all_to_all.91, bf16[1440,768]{1,0:T(8,128)(2,1)} %reshape_reshape.3, f32[1440,720]{1,0:T(8,128)} %get-tuple-element.20, f32[1440,720]{1,0:T(8,128)} %get-tuple-element.19), kind=kOutput, calls=%fused_computation.26 | convolution fusion | flops 3194588160 | bytes 14929920 | tf_op jit(solution)/shard_map/dot_general | solution.py:124
  491.5 62.8 %all_to_all.124 = bf16[16,90,768]{2,1,0:T(8,128)(2,1)S(1)} all-to-all(bf16[16,90,768]{2,1,0:T(8,128)(2,1)S(1)} %all_to_all.110), channel_id=1, replica_groups=mesh['lat'=4,'lon'=16,'ch'=4] {'lon'}, dimensions={0} | all-to-all | bytes 4423680 | tf_op jit(solution)/shard_map/all_to_all | solution.py:127
  (70 shorter events, 89.6 us)
Async XLA Ops:
  4.5 66.6 %all-to-all-start = ((bf16[90,16,768]{2,0,1:T(8,128)(2,1)}), bf16[90,16,768]{2,0,1:T(8,128)(2,1)S(1)}, u32[]{:S(2)}, u32[]{:S(2)}) async-start(bf16[90,16,768]{2,0,1:T(8,128)(2,1)} %copy.132), calls=%async_computation | async-start | bytes 4718592 | tf_op jit(solution)/shard_map/all_to_all | solution.py:109
  52.3 3.4 copy-start.1
  52.3 7.3 %copy-start = (f32[1440,1440]{1,0:T(8,128)}, f32[1440,1440]{1,0:T(8,128)S(1)}, u32[]{:S(2)}) copy-start(f32[1440,1440]{1,0:T(8,128)S(1)} %get-tuple-element.23) | copy-start | bytes 24883204
  155.4 30.9 %all-to-all-start.2 = ((bf16[2,45,128,96]{2,0,1,3:T(2,128)(2,1)}), bf16[2,45,128,96]{2,0,1,3:T(2,128)(2,1)S(1)}, u32[]{:S(2)}, u32[]{:S(2)}) async-start(bf16[2,45,128,96]{2,0,1,3:T(2,128)(2,1)} %copy.135), calls=%async_computation.2 | async-start | bytes 4423680 | tf_op jit(solution)/shard_map/all_to_all | solution.py:86
  203.9 17.5 %copy-start.3 = (bf16[1,2,96,96]{3,2,1,0:T(8,128)(2,1)S(1)}, bf16[1,2,96,96]{3,2,1,0:T(8,128)(2,1)}, u32[]{:S(2)}) copy-start(bf16[1,2,96,96]{3,2,1,0:T(8,128)(2,1)} %param.6) | copy-start | bytes 110596
  217.4 4.2 copy-start.4
  217.4 30.8 %all-to-all-start.3 = ((bf16[4,2,138240]{2,1,0:T(2,128)(2,1)}), bf16[4,2,138240]{2,1,0:T(2,128)(2,1)S(1)}, u32[]{:S(2)}, u32[]{:S(2)}) async-start(bf16[4,2,138240]{2,1,0:T(2,128)(2,1)} %reshape.177), calls=%async_computation.3 | async-start | bytes 4423680 | tf_op jit(solution)/shard_map/all_to_all | solution.py:90
  267.5 7.8 %copy-start.5 = (f32[1,2,96]{2,1,0:T(2,128)S(1)}, f32[1,2,96]{2,1,0:T(2,128)}, u32[]{:S(2)}) copy-start(f32[1,2,96]{2,1,0:T(2,128)} %param.7) | copy-start | bytes 2308
  267.5 8.6 %copy-start.6 = (f32[1,2,96]{2,1,0:T(2,128)S(1)}, f32[1,2,96]{2,1,0:T(2,128)}, u32[]{:S(2)}) copy-start(f32[1,2,96]{2,1,0:T(2,128)} %param.9) | copy-start | bytes 2308
  415.8 57.5 %all-to-all-start.6 = ((bf16[16,2,45,768]{3,1,2,0:T(2,128)(2,1)}), bf16[16,2,45,768]{3,1,2,0:T(2,128)(2,1)S(1)}, u32[]{:S(2)}, u32[]{:S(2)}) async-start(bf16[16,2,45,768]{3,1,2,0:T(2,128)(2,1)} %copy.145), calls=%async_computation.6 | async-start | bytes 4423680 | tf_op jit(solution)/shard_map/all_to_all | solution.py:121
  473.3 1.4 copy-start.2
